TPU v7x, 32 devices: a whole 2x2x4 slice. The times are simulated.
32 devices in a mesh: groups: 2 (over y), strip: 16 (over z, x, core).
Axes of the slice: x: 2, y: 2, z: 4, core: 2. Of those that a mesh axis runs over, the one named last changes fastest.
Arguments:
- bands: bfloat16 [64, 2048], P(('groups', 'strip')), parts along dimension 0, may hold values from -6 to 6
- target: bfloat16 [64, 2048], P('groups', 'strip'), parts along dimension 0, may hold values from -6 to 6
- w_in: bfloat16 [32, 128], replicated, may hold values from -1 to 1
- w_conv: bfloat16 [3, 3, 4, 32, 32], replicated, may hold values from -0.375 to 0.375
- w_track: bfloat16 [3, 3, 128, 128], replicated, may hold values from -0.3125 to 0.3125
- w_out: bfloat16 [128, 32], replicated, may hold values from -0.5 to 0.5
- table: float32 [64, 32], replicated, may hold values from -6 to 6
- dilation: int32 [3], replicated, may hold values from 1 to 8, as said below
- detector: int32 [128], P(('groups', 'strip')), parts along dimension 0, may hold values from 0 to 63
- flags: int32 [128], P(('groups', 'strip')), parts along dimension 0, may hold values 0 or 1
Outputs:
- prediction: bfloat16 [64, 2048], P('groups', 'strip'), parts along dimension 0
- grad_in: float32 [64, 128], P('groups'), parts along dimension 0
- grad_conv: float32 [6, 3, 4, 32, 32], P('groups'), parts along dimension 0
- grad_track: float32 [6, 3, 128, 128], P('groups'), parts along dimension 0
- grad_out: float32 [256, 32], P('groups'), parts along dimension 0
- grad_table: float32 [128, 32], P('groups'), parts along dimension 0
There are 2 independent parts, one for each index of `groups`. A program takes and returns all parts, laid end to end along the dimension named above; an argument that names none is the same for every part. Nothing has to cross between parts.
Inputs may be any that keep to these rules, and one draw needn't show every extreme that they name: `dilation`: each entry is 1 to 8, and one entry equals 8.
All inputs are finite; a program needn't handle non-finite values. No bound on the sum of `flags` on one device may be relied on, other than what follows from the above.
Results may differ from a plain program's by a relative error of at most 0.01.
Values may be sent and summed in bfloat16 or wider, within the bound.
No kernel may reach another device: no remote copies, remote signals or barrier semaphores. Data moves between devices by JAX's collectives and lax.ppermute only.
A program may use at most 64 MiB of HBM per device.

v0:
```python
import math
import jax
import jax.numpy as jnp
from jax import lax
from jax.sharding import PartitionSpec as P


def with_halo(x, sides, width):
    for axis, dim in sides:
        size, length = (lax.axis_size(axis), x.shape[dim])
        up = [(i, (i + 1) % size) for i in range(size - 1)]
        down = [(j, i) for i, j in up]
        last = lax.slice_in_dim(x, length - width, length, axis=dim)
        initial = lax.slice_in_dim(x, 0, width, axis=dim)
        before = lax.ppermute(last, axis, up)
        after = lax.ppermute(initial, axis, down)
        x = jnp.concatenate([before, x, after], axis=dim)
    return x


def silu_slope(preact):
    sigmoid_val = jax.nn.sigmoid(preact)
    return sigmoid_val * (1.0 + preact * (1.0 - sigmoid_val))


def block_diagonal(weight):
    groups = weight.shape[2]
    width = weight.shape[3]
    identity = jnp.eye(groups, dtype=weight.dtype)
    spread = weight[:, :, :, :, None, :] * identity[None, None, :, None, :, None]
    return spread.reshape(3, 3, groups * width, groups * width)


def conv_forward(padded, dense_weight):
    row_count = padded.shape[0] - 2
    col_count = padded.shape[1] - 2
    chan_count = padded.shape[2]
    summed = jnp.zeros((row_count * col_count, dense_weight.shape[3]), jnp.float32)
    for i in range(3):
        for j in range(3):
            window = padded[i : i + row_count, j : j + col_count].reshape(-1, chan_count)
            summed = summed + jnp.dot(
                window, dense_weight[i, j], preferred_element_type=jnp.float32
            )
    return summed.reshape(row_count, col_count, -1)


def conv_transpose(padded_grad, dense_weight):
    row_count = padded_grad.shape[0] - 2
    col_count = padded_grad.shape[1] - 2
    chan_count = padded_grad.shape[2]
    summed = jnp.zeros((row_count * col_count, dense_weight.shape[2]), jnp.float32)
    for i in range(3):
        for j in range(3):
            window = padded_grad[2 - i : 2 - i + row_count, 2 - j : 2 - j + col_count].reshape(
                -1, chan_count
            )
            summed = summed + jnp.dot(
                window, dense_weight[i, j].T, preferred_element_type=jnp.float32
            )
    return summed.reshape(row_count, col_count, -1)


def conv_weight_grad(padded, gradient, groups):
    row_count = gradient.shape[0]
    col_count = gradient.shape[1]
    chan_count = gradient.shape[2]
    width = chan_count // groups
    contract = (((0,), (0,)), ((), ()))
    flat_out = gradient.reshape(-1, chan_count)
    rows_of_taps = []
    for i in range(3):
        taps = []
        for j in range(3):
            window = padded[i : i + row_count, j : j + col_count].reshape(-1, chan_count)
            full = lax.dot_general(window, flat_out, contract, preferred_element_type=jnp.float32)
            taps.append(
                jnp.stack(
                    [
                        full[g * width : (g + 1) * width, g * width : (g + 1) * width]
                        for g in range(groups)
                    ]
                )
            )
        rows_of_taps.append(jnp.stack(taps))
    return jnp.stack(rows_of_taps)


def shifted(source, offset, margin):
    padded = jnp.pad(source, ((margin, margin), (0, 0), (0, 0)))
    return lax.dynamic_slice_in_dim(padded, margin + offset, source.shape[0], 0)


def project_pixels(pixels, w_in):
    flat = jnp.dot(pixels.reshape(-1, pixels.shape[2]), w_in, preferred_element_type=jnp.float32)
    return flat.astype(jnp.bfloat16).reshape(pixels.shape[0], pixels.shape[1], w_in.shape[1])


def column_work(
    features, target_block, w_track, w_out, table, dilation, detector, flags, loss_scale
):
    row_count, col_count, chan_count = features.shape
    band_count = w_out.shape[1]
    layers = w_track.shape[0]
    margin = row_count // 4
    contract = (((0,), (0,)), ((), ()))
    selector = (detector[:, None] == jnp.arange(table.shape[0], dtype=jnp.int32)[None, :]).astype(
        jnp.float32
    )
    flag_values = flags.astype(jnp.float32)
    offsets = flag_values[:, None] * jnp.dot(selector, table, precision=lax.Precision.HIGHEST)
    activations = [features]
    preacts = []
    current = features
    for layer_index in range(layers):
        spacing = dilation[layer_index]
        preact = jnp.zeros((row_count * col_count, chan_count), jnp.float32)
        for tap_index in range(3):
            moved_rows = shifted(current, (tap_index - 1) * spacing, margin)
            preact = preact + jnp.dot(
                moved_rows.reshape(-1, chan_count),
                w_track[layer_index, tap_index],
                preferred_element_type=jnp.float32,
            )
        preact = preact.reshape(row_count, col_count, chan_count)
        current = (current.astype(jnp.float32) + jax.nn.silu(preact)).astype(jnp.bfloat16)
        preacts.append(preact)
        activations.append(current)
    raw_output = (
        jnp.dot(current.reshape(-1, chan_count), w_out, preferred_element_type=jnp.float32).reshape(
            row_count, col_count, band_count
        )
        + offsets[None]
    )
    prediction = raw_output.astype(jnp.bfloat16)
    residue = (
        prediction.astype(jnp.float32)
        - target_block.reshape(row_count, col_count, band_count).astype(jnp.float32)
    ) * loss_scale
    residue_b = residue.astype(jnp.bfloat16)
    grad_out = lax.dot_general(
        current.reshape(-1, chan_count),
        residue_b.reshape(-1, band_count),
        contract,
        preferred_element_type=jnp.float32,
    )
    column_sums = jnp.sum(residue, axis=0) * flag_values[:, None]
    grad_table = jnp.dot(selector.T, column_sums, precision=lax.Precision.HIGHEST)
    backward = jnp.dot(
        residue_b.reshape(-1, band_count), w_out.T, preferred_element_type=jnp.float32
    ).reshape(row_count, col_count, chan_count)
    track_grads = [None] * layers
    for layer_index in reversed(range(layers)):
        spacing = dilation[layer_index]
        gate_grad = (backward * silu_slope(preacts[layer_index])).astype(jnp.bfloat16)
        flat_grad = gate_grad.reshape(-1, chan_count)
        tap_grads = []
        for tap_index in range(3):
            moved_rows = shifted(activations[layer_index], (tap_index - 1) * spacing, margin)
            tap_grads.append(
                lax.dot_general(
                    moved_rows.reshape(-1, chan_count),
                    flat_grad,
                    contract,
                    preferred_element_type=jnp.float32,
                )
            )
            pulled = jnp.dot(
                flat_grad, w_track[layer_index, tap_index].T, preferred_element_type=jnp.float32
            ).reshape(row_count, col_count, chan_count)
            backward = backward + shifted(pulled, (1 - tap_index) * spacing, margin)
        track_grads[layer_index] = jnp.stack(tap_grads)
    return (
        backward.astype(jnp.bfloat16),
        prediction.reshape(row_count, col_count * band_count),
        jnp.stack(track_grads),
        grad_out,
        grad_table,
    )


def body(bands, target, w_in, w_conv, w_track, w_out, table, dilation, detector, flags):
    band_count = w_in.shape[0]
    chan_count = w_in.shape[1]
    groups = w_conv.shape[2]
    device_count = lax.axis_size("strip")
    dense_conv = block_diagonal(w_conv)
    row_count = bands.shape[0]
    col_count = bands.shape[1] // band_count
    pixels = bands.reshape(row_count, col_count, band_count)
    projected = project_pixels(pixels, w_in)
    padded = with_halo(projected, (("strip", 0),), 1)
    padded = jnp.pad(padded, ((0, 0), (1, 1), (0, 0)))
    spatial = conv_forward(padded, dense_conv)
    features = (projected.astype(jnp.float32) + jax.nn.silu(spatial)).astype(jnp.bfloat16)
    feature_cols = lax.all_to_all(features, "strip", split_axis=1, concat_axis=0, tiled=True)
    loss_scale = 1.0 / math.sqrt(feature_cols.shape[0] * feature_cols.shape[1] * device_count)
    feature_grad, prediction, grad_track, grad_out, grad_table = column_work(
        feature_cols, target, w_track, w_out, table, dilation, detector, flags, loss_scale
    )
    local_grad = lax.all_to_all(feature_grad, "strip", split_axis=0, concat_axis=1, tiled=True)
    mixed_grad = (local_grad.astype(jnp.float32) * silu_slope(spatial)).astype(jnp.bfloat16)
    grad_pad = with_halo(mixed_grad, (("strip", 0),), 1)
    grad_pad = jnp.pad(grad_pad, ((0, 0), (1, 1), (0, 0)))
    lifted = (local_grad.astype(jnp.float32) + conv_transpose(grad_pad, dense_conv)).astype(
        jnp.bfloat16
    )
    grad_conv = conv_weight_grad(padded, mixed_grad, groups)
    contract = (((0,), (0,)), ((), ()))
    grad_in = lax.dot_general(
        pixels.reshape(-1, band_count),
        lifted.reshape(-1, chan_count),
        contract,
        preferred_element_type=jnp.float32,
    )
    grad_in, grad_conv, grad_track, grad_out, grad_table = lax.psum(
        (grad_in, grad_conv, grad_track, grad_out, grad_table), "strip"
    )
    return (prediction, grad_in, grad_conv, grad_track, grad_out, grad_table)


def solution(mesh):
    placed = (
        P(("groups", "strip"), None),
        P("groups", "strip"),
        P(),
        P(),
        P(),
        P(),
        P(),
        P(),
        P(("groups", "strip")),
        P(("groups", "strip")),
    )
    return jax.shard_map(
        body,
        mesh=mesh,
        in_specs=placed,
        out_specs=(
            P("groups", "strip"),
            P("groups", None),
            P("groups", None, None, None, None),
            P("groups", None, None, None),
            P("groups", None),
            P("groups", None),
        ),
        check_vma=False,
    )
```

profile of v0, /device:TPU:0, one launch (start us, length us, event | category | flops | bytes accessed | tf_op | source)
XLA Modules:
  0.0 162.6 jit_solution(9685957175195041190)
XLA Ops:
  7.2 0.8 reshape_reshape.4
  8.0 0.8 convolution_convert_fusion
  8.8 1.3 collective-permute-start.1
  10.1 3.0 %collective-permute-start = (bf16[1,64,128]{2,1,0:T(8,128)(2,1)S(1)}, bf16[1,64,128]{2,1,0:T(8,128)(2,1)S(1)}, u32[]{:S(2)}, u32[]{:S(2)}) collective-permute-start(bf16[1,64,128]{2,1,0:T(8,128)(2,1)S(1)} %get-tuple-element.73), channel_id=1, source_target_pairs={{0,1},{1,2},{2,3},{3,4},{4,5},{5,6},{6,7},{7,8},{8,9},{9,10},{10,1... | collective-permute-start | bytes 49160 | tf_op jit(solution)/shard_map/ppermute | solution.py:15
  13.2 0.7 convert_element_type.177
  13.8 1.5 mul.138
  15.3 0.6 mul.139
  17.8 0.6 copy.53
  18.5 8.0 %all-to-all-start = ((bf16[2,64,128]{2,0,1:T(2,128)(2,1)}), bf16[2,64,128]{2,0,1:T(2,128)(2,1)S(1)}, u32[]{:S(2)}, u32[]{:S(2)}) async-start(bf16[2,64,128]{2,0,1:T(2,128)(2,1)} %copy.53), calls=%async_computation | async-start | bytes 65536 | tf_op jit(solution)/shard_map/all_to_all | solution.py:196
  26.4 0.6 fusion.102
  35.4 0.2 multiply_convert_fusion.3
  35.9 0.2 multiply_convert_fusion.2
  36.4 0.2 convolution_bitcast_fusion.18
  38.3 0.6 copy.73
  38.9 6.0 %all-to-all-start.1 = ((bf16[32,4,128]{2,1,0:T(4,128)(2,1)}), bf16[32,4,128]{2,1,0:T(4,128)(2,1)S(1)}, u32[]{:S(2)}, u32[]{:S(2)}) async-start(bf16[32,4,128]{2,1,0:T(4,128)(2,1)} %copy.73), calls=%async_computation.1 | async-start | bytes 65536 | tf_op jit(solution)/shard_map/all_to_all | solution.py:201
  44.9 0.3 fusion.80
  45.2 0.2 convolution_bitcast_fusion.9
  45.5 0.9 pad_maximum_fusion.1
  46.3 0.7 reshape.252
  47.0 4.5 %all-to-all-done.1 = bf16[32,4,128]{2,1,0:T(4,128)(2,1)S(1)} async-done(((bf16[32,4,128]{2,1,0:T(4,128)(2,1)}), bf16[32,4,128]{2,1,0:T(4,128)(2,1)S(1)}, u32[]{:S(2)}, u32[]{:S(2)}) %all-to-all-start.1) | async-done | bytes 32800 | tf_op jit(solution)/shard_map/all_to_all | solution.py:201
  51.6 0.2 convolution_bitcast_fusion.11
  52.0 0.2 convolution_bitcast_fusion.13
  52.7 1.3 collective-permute-start.3
  54.0 3.0 %collective-permute-start.2 = (bf16[1,64,128]{2,1,0:T(8,128)(2,1)S(1)}, bf16[1,64,128]{2,1,0:T(8,128)(2,1)S(1)}, u32[]{:S(2)}, u32[]{:S(2)}) collective-permute-start(bf16[1,64,128]{2,1,0:T(8,128)(2,1)S(1)} %get-tuple-element.61), channel_id=1, source_target_pairs={{0,1},{1,2},{2,3},{3,4},{4,5},{5,6},{6,7},{7,8},{8,9},{9,10},{10,1... | collective-permute-start | bytes 49160 | tf_op jit(solution)/shard_map/ppermute | solution.py:15
  57.2 0.2 convolution_bitcast_fusion
  58.2 0.2 convolution_bitcast_fusion.1
  58.6 0.9 pad_maximum_fusion
  60.8 0.3 fusion.10
  61.2 59.5 %all-reduce.11 = (f32[32,128]{1,0:T(8,128)}, f32[128,32]{0,1:T(8,128)}, f32[64,32]{0,1:T(8,128)}) all-reduce(f32[32,128]{1,0:T(8,128)S(1)} %fusion.10, f32[128,32]{0,1:T(8,128)S(1)} %convolution_bitcast_fusion.18, f32[64,32]{0,1:T(8,128)S(1)} %fusion.80), channel_id=1, replica_groups=mesh['groups'=2,'strip'=16] {'strip'}, use_global_device_ids=true, to_apply=%region_0.1 | all-reduce | flops 10240 | bytes 81920 | tf_op jit(solution)/shard_map/psum | solution.py:216
  120.7 32.3 %all-reduce.15.cloned.1.call-done = (f32[3,3,4,32,32]{4,3,2,1,0:T(8,128)}, f32[3,3,128,128]{3,2,1,0:T(8,128)}) async-done(((f32[3,3,4,32,32]{4,3,2,1,0:T(8,128)}, f32[3,3,128,128]{3,2,1,0:T(8,128)}), (f32[3,3,4,32,32]{4,3,2,1,0:T(8,128)}, f32[3,3,128,128]{3,2,1,0:T(8,128)})) %all-reduce.15.cloned.1.call-update) | async-done | bytes 737296 | tf_op jit(solution)/shard_map/psum | solution.py:216
  152.9 2.0 %copy.107 = f32[3,3,4,32,32]{4,3,2,1,0:T(8,128)} copy(f32[3,3,4,32,32]{4,3,2,1,0:T(8,128)} %get-tuple-element.100) | data formatting | bytes 294912
  154.9 0.8 copy.108
  (122 shorter events, 9.7 us)
Async XLA Ops:
  7.2 9.0 %copy-start = (f32[64,32]{0,1:T(8,128)S(1)}, f32[64,32]{0,1:T(8,128)}, u32[]{:S(2)}) copy-start(f32[64,32]{0,1:T(8,128)} %param.16) | copy-start | bytes 24580
  8.8 7.6 %collective-permute-start.1 = (bf16[1,64,128]{2,1,0:T(8,128)(2,1)S(1)}, bf16[1,64,128]{2,1,0:T(8,128)(2,1)S(1)}, u32[]{:S(2)}, u32[]{:S(2)}) collective-permute-start(bf16[1,64,128]{2,1,0:T(8,128)(2,1)S(1)} %get-tuple-element.74), channel_id=1, source_target_pairs={{1,0},{2,1},{3,2},{4,3},{5,4},{6,5},{7,6},{8,7},{9,8},{10,9},{11,1... | collective-permute-start | bytes 49160 | tf_op jit(solution)/shard_map/ppermute | solution.py:16
  10.1 6.3 %collective-permute-start = (bf16[1,64,128]{2,1,0:T(8,128)(2,1)S(1)}, bf16[1,64,128]{2,1,0:T(8,128)(2,1)S(1)}, u32[]{:S(2)}, u32[]{:S(2)}) collective-permute-start(bf16[1,64,128]{2,1,0:T(8,128)(2,1)S(1)} %get-tuple-element.73), channel_id=1, source_target_pairs={{0,1},{1,2},{2,3},{3,4},{4,5},{5,6},{6,7},{7,8},{8,9},{9,10},{10,1... | collective-permute-start | bytes 49160 | tf_op jit(solution)/shard_map/ppermute | solution.py:15
  15.3 0.9 copy-start.6
  16.4 10.0 %copy-start.5 = (s32[3]{0:T(128)S(1)}, s32[3]{0:T(128)}, u32[]{:S(2)}) copy-start(s32[3]{0:T(128)} %param.17) | copy-start | bytes 40
  16.5 16.4 %copy-start.3 = (bf16[32,128]{1,0:T(8,128)(2,1)S(1)}, bf16[32,128]{1,0:T(8,128)(2,1)}, u32[]{:S(2)}) copy-start(bf16[32,128]{1,0:T(8,128)(2,1)} %param.11) | copy-start | bytes 24580
  16.8 16.5 %copy-start.1 = (bf16[3,3,128,128]{3,2,1,0:T(8,128)(2,1)S(1)}, bf16[3,3,128,128]{3,2,1,0:T(8,128)(2,1)}, u32[]{:S(2)}) copy-start(bf16[3,3,128,128]{3,2,1,0:T(8,128)(2,1)} %param.14) | copy-start | bytes 884740
  18.5 14.6 %all-to-all-start = ((bf16[2,64,128]{2,0,1:T(2,128)(2,1)}), bf16[2,64,128]{2,0,1:T(2,128)(2,1)S(1)}, u32[]{:S(2)}, u32[]{:S(2)}) async-start(bf16[2,64,128]{2,0,1:T(2,128)(2,1)} %copy.53), calls=%async_computation | async-start | bytes 65536 | tf_op jit(solution)/shard_map/all_to_all | solution.py:196
  33.8 1.1 copy-start.4
  38.9 12.6 %all-to-all-start.1 = ((bf16[32,4,128]{2,1,0:T(4,128)(2,1)}), bf16[32,4,128]{2,1,0:T(4,128)(2,1)S(1)}, u32[]{:S(2)}, u32[]{:S(2)}) async-start(bf16[32,4,128]{2,1,0:T(4,128)(2,1)} %copy.73), calls=%async_computation.1 | async-start | bytes 65536 | tf_op jit(solution)/shard_map/all_to_all | solution.py:201
  44.9 108.0 %all-reduce.15.cloned.1.call-start = ((), (), s32[]{:S(2)}) async-start(), calls=%async_computation.2 | async-start | bytes 2359296 | tf_op jit(solution)/shard_map/psum | solution.py:216
  52.7 6.8 %collective-permute-start.3 = (bf16[1,64,128]{2,1,0:T(8,128)(2,1)S(1)}, bf16[1,64,128]{2,1,0:T(8,128)(2,1)S(1)}, u32[]{:S(2)}, u32[]{:S(2)}) collective-permute-start(bf16[1,64,128]{2,1,0:T(8,128)(2,1)S(1)} %get-tuple-element.62), channel_id=1, source_target_pairs={{1,0},{2,1},{3,2},{4,3},{5,4},{6,5},{7,6},{8,7},{9,8},{10,9},{11,1... | collective-permute-start | bytes 49160 | tf_op jit(solution)/shard_map/ppermute | solution.py:16
  54.0 5.5 %collective-permute-start.2 = (bf16[1,64,128]{2,1,0:T(8,128)(2,1)S(1)}, bf16[1,64,128]{2,1,0:T(8,128)(2,1)S(1)}, u32[]{:S(2)}, u32[]{:S(2)}) collective-permute-start(bf16[1,64,128]{2,1,0:T(8,128)(2,1)S(1)} %get-tuple-element.61), channel_id=1, source_target_pairs={{0,1},{1,2},{2,3},{3,4},{4,5},{5,6},{6,7},{7,8},{8,9},{9,10},{10,1... | collective-permute-start | bytes 49160 | tf_op jit(solution)/shard_map/ppermute | solution.py:15
  152.9 2.0 %copy-start.2 = (f32[3,3,128,128]{3,2,1,0:T(8,128)S(1)}, f32[3,3,128,128]{3,2,1,0:T(8,128)}, u32[]{:S(2)}) copy-start(f32[3,3,128,128]{3,2,1,0:T(8,128)} %get-tuple-element.101) | copy-start | bytes 1769476
Sparse Core Ops, SparseCore 0:
  59.6 93.2 all-reduce.14
where the time goes:
time: 163 us
  blocking collectives  59.5 us (37%)
  waiting for transfers between devices  36.8 us (23%)
  starting transfers between devices  22.6 us (14%)
  between operations  20.5 us (13%)
  matrix products  10.5 us (6%)
  local copies, waits for them, and re-layouts  9.7 us (6%)
  other arithmetic  2.92 us (2%)
    psum x1, blocking collectives, body(): lax.psum((grad_in, grad_conv, grad_track, grad_out, grad_table), 'strip')  59.5 us
    psum x1, waiting for transfers between devices, body(): lax.psum((grad_in, grad_conv, grad_track, grad_out, grad_table), 'strip')  32.3 us
    all_to_all x1, starting transfers between devices, body(): lax.all_to_all(features, 'strip', split_axis=1, concat_axis=0, tiled=True)  7.95 us
    ppermute x2, starting transfers between devices, with_halo(): before = lax.ppermute(last, axis, up)  6.06 us
    all_to_all x1, starting transfers between devices, body(): lax.all_to_all(feature_grad, 'strip', split_axis=0, concat_axis=1, tiled=...  5.97 us
    all_to_all x1, waiting for transfers between devices, body(): lax.all_to_all(feature_grad, 'strip', split_axis=0, concat_axis=1, tiled=...  4.5 us
  transfers between devices with their start and end apart: 7, of which 2 were waited for; matrix products, arithmetic and copies ran while one was open for 6% of the time, Pallas kernels for 0%

commit v1 on v0

--- a/solution.py
+++ b/solution.py
@@ -198,7 +198,12 @@
     feature_grad, prediction, grad_track, grad_out, grad_table = column_work(
         feature_cols, target, w_track, w_out, table, dilation, detector, flags, loss_scale
     )
-    local_grad = lax.all_to_all(feature_grad, "strip", split_axis=0, concat_axis=1, tiled=True)
+    local_grad = jnp.concatenate(
+        lax.all_to_all(
+            jnp.stack(jnp.split(feature_grad, lax.axis_size("strip"), axis=0)), "strip", 0, 0
+        ),
+        axis=1,
+    )
     mixed_grad = (local_grad.astype(jnp.float32) * silu_slope(spatial)).astype(jnp.bfloat16)
     grad_pad = with_halo(mixed_grad, (("strip", 0),), 1)
     grad_pad = jnp.pad(grad_pad, ((0, 0), (1, 1), (0, 0)))

time: 163 us -> 172 us (1.055)
  local copies, waits for them, and re-layouts: 9.7 us -> 18.4 us
    unnamed x16 -> x31, local copies, waits for them, and re-layouts: 2.83 us -> 11.5 us
where the time goes in v1:
time: 172 us; the launch traced here: 171 us
  blocking collectives  59.5 us (35%)
  waiting for transfers between devices  36.8 us (21%)
  starting transfers between devices  22.6 us (13%)
  between operations  20.6 us (12%)
  local copies, waits for them, and re-layouts  18.4 us (11%)
  matrix products  10.5 us (6%)
  other arithmetic  2.9 us (2%)
    psum x1, blocking collectives, body(): lax.psum((grad_in, grad_conv, grad_track, grad_out, grad_table), 'strip')  59.5 us
    psum x1, waiting for transfers between devices, body(): lax.psum((grad_in, grad_conv, grad_track, grad_out, grad_table), 'strip')  32.3 us
    unnamed x31, local copies, waits for them, and re-layouts  11.5 us
    all_to_all x1, starting transfers between devices, body(): lax.all_to_all(features, 'strip', split_axis=1, concat_axis=0, tiled=True)  7.95 us
    ppermute x2, starting transfers between devices, with_halo(): before = lax.ppermute(last, axis, up)  6.06 us
    all_to_all x1, starting transfers between devices, body(): lax.all_to_all(jnp.stack(jnp.split(feature_grad, lax.axis_size('strip'),...  5.97 us
    all_to_all x1, waiting for transfers between devices, body(): lax.all_to_all(jnp.stack(jnp.split(feature_grad, lax.axis_size('strip'),...  4.5 us
  transfers between devices with their start and end apart: 7, of which 2 were waited for; matrix products, arithmetic and copies ran while one was open for 6% of the time, Pallas kernels for 0%

profile of v1, /device:TPU:0, one launch (start us, length us, event | category | flops | bytes accessed | tf_op | source)
XLA Modules:
  0.0 171.3 jit_solution(11528897608488509562)
XLA Ops:
  7.2 0.8 reshape_reshape.4
  8.0 0.8 convolution_convert_fusion
  8.8 1.3 collective-permute-start.1
  10.1 3.0 %collective-permute-start = (bf16[1,64,128]{2,1,0:T(8,128)(2,1)S(1)}, bf16[1,64,128]{2,1,0:T(8,128)(2,1)S(1)}, u32[]{:S(2)}, u32[]{:S(2)}) collective-permute-start(bf16[1,64,128]{2,1,0:T(8,128)(2,1)S(1)} %get-tuple-element.89), channel_id=1, source_target_pairs={{0,1},{1,2},{2,3},{3,4},{4,5},{5,6},{6,7},{7,8},{8,9},{9,10},{10,1... | collective-permute-start | bytes 49160 | tf_op jit(solution)/shard_map/ppermute | solution.py:15
  13.2 0.7 convert_element_type.172
  13.8 1.5 mul.138
  17.8 0.6 copy.1152
  18.5 8.0 %all-to-all-start = ((bf16[2,64,128]{2,0,1:T(2,128)(2,1)}), bf16[2,64,128]{2,0,1:T(2,128)(2,1)S(1)}, u32[]{:S(2)}, u32[]{:S(2)}) async-start(bf16[2,64,128]{2,0,1:T(2,128)(2,1)} %copy.1152), calls=%async_computation | async-start | bytes 65536 | tf_op jit(solution)/shard_map/all_to_all | solution.py:196
  26.4 0.6 fusion.102
  38.3 0.6 constant_dynamic-update-slice_fusion.15
  38.9 0.6 constant_dynamic-update-slice_fusion.14
  39.5 0.6 constant_dynamic-update-slice_fusion.13
  40.1 0.6 constant_dynamic-update-slice_fusion.12
  40.6 0.6 constant_dynamic-update-slice_fusion.11
  41.2 0.6 constant_dynamic-update-slice_fusion.10
  41.8 0.6 constant_dynamic-update-slice_fusion.9
  42.4 0.6 constant_dynamic-update-slice_fusion.8
  43.0 0.6 constant_dynamic-update-slice_fusion.7
  43.5 0.6 constant_dynamic-update-slice_fusion.6
  44.1 0.6 constant_dynamic-update-slice_fusion.5
  45.9 0.6 constant_dynamic-update-slice_fusion.2
  47.6 6.0 %all-to-all-start.1 = ((bf16[16,2,4,128]{3,2,1,0:T(4,128)(2,1)}), bf16[16,2,4,128]{3,2,1,0:T(4,128)(2,1)S(1)}, u32[]{:S(2)}, u32[]{:S(2)}) async-start(bf16[16,2,4,128]{3,2,1,0:T(4,128)(2,1)} %constant_dynamic-update-slice_fusion), calls=%async_computation.1 | async-start | bytes 65536 | tf_op jit(solution)/shard_map/all_to_all | solution.py:202
  54.2 0.9 pad_maximum_fusion.1
  55.0 0.7 reshape.248
  55.7 4.5 %all-to-all-done.1 = bf16[16,2,4,128]{3,2,1,0:T(4,128)(2,1)S(1)} async-done(((bf16[16,2,4,128]{3,2,1,0:T(4,128)(2,1)}), bf16[16,2,4,128]{3,2,1,0:T(4,128)(2,1)S(1)}, u32[]{:S(2)}, u32[]{:S(2)}) %all-to-all-start.1) | async-done | bytes 32800 | tf_op jit(solution)/shard_map/all_to_all | solution.py:202
  61.5 1.3 collective-permute-start.3
  62.8 3.0 %collective-permute-start.2 = (bf16[1,64,128]{2,1,0:T(8,128)(2,1)S(1)}, bf16[1,64,128]{2,1,0:T(8,128)(2,1)S(1)}, u32[]{:S(2)}, u32[]{:S(2)}) collective-permute-start(bf16[1,64,128]{2,1,0:T(8,128)(2,1)S(1)} %get-tuple-element.61), channel_id=1, source_target_pairs={{0,1},{1,2},{2,3},{3,4},{4,5},{5,6},{6,7},{7,8},{8,9},{9,10},{10,1... | collective-permute-start | bytes 49160 | tf_op jit(solution)/shard_map/ppermute | solution.py:15
  67.4 0.9 pad_maximum_fusion
  69.9 59.5 %all-reduce.11 = (f32[32,128]{1,0:T(8,128)}, f32[128,32]{0,1:T(8,128)}, f32[64,32]{0,1:T(8,128)}) all-reduce(f32[32,128]{1,0:T(8,128)S(1)} %fusion.10, f32[128,32]{0,1:T(8,128)S(1)} %convolution_bitcast_fusion.18, f32[64,32]{0,1:T(8,128)S(1)} %fusion.79), channel_id=1, replica_groups=mesh['groups'=2,'strip'=16] {'strip'}, use_global_device_ids=true, to_apply=%region_0.1 | all-reduce | flops 10240 | bytes 81920 | tf_op jit(solution)/shard_map/psum | solution.py:221
  129.4 32.3 %all-reduce.15.cloned.1.call-done = (f32[3,3,4,32,32]{4,3,2,1,0:T(8,128)}, f32[3,3,128,128]{3,2,1,0:T(8,128)}) async-done(((f32[3,3,4,32,32]{4,3,2,1,0:T(8,128)}, f32[3,3,128,128]{3,2,1,0:T(8,128)}), (f32[3,3,4,32,32]{4,3,2,1,0:T(8,128)}, f32[3,3,128,128]{3,2,1,0:T(8,128)})) %all-reduce.15.cloned.1.call-update) | async-done | bytes 737296 | tf_op jit(solution)/shard_map/psum | solution.py:221
  161.7 2.0 %copy.1260 = f32[3,3,4,32,32]{4,3,2,1,0:T(8,128)} copy(f32[3,3,4,32,32]{4,3,2,1,0:T(8,128)} %get-tuple-element.116) | data formatting | bytes 294912
  163.6 0.8 copy.1261
  (140 shorter events, 14.7 us)
Async XLA Ops:
  7.2 9.0 %copy-start = (f32[64,32]{0,1:T(8,128)S(1)}, f32[64,32]{0,1:T(8,128)}, u32[]{:S(2)}) copy-start(f32[64,32]{0,1:T(8,128)} %param.16) | copy-start | bytes 24580
  8.8 7.6 %collective-permute-start.1 = (bf16[1,64,128]{2,1,0:T(8,128)(2,1)S(1)}, bf16[1,64,128]{2,1,0:T(8,128)(2,1)S(1)}, u32[]{:S(2)}, u32[]{:S(2)}) collective-permute-start(bf16[1,64,128]{2,1,0:T(8,128)(2,1)S(1)} %get-tuple-element.90), channel_id=1, source_target_pairs={{1,0},{2,1},{3,2},{4,3},{5,4},{6,5},{7,6},{8,7},{9,8},{10,9},{11,1... | collective-permute-start | bytes 49160 | tf_op jit(solution)/shard_map/ppermute | solution.py:16
  10.1 6.3 %collective-permute-start = (bf16[1,64,128]{2,1,0:T(8,128)(2,1)S(1)}, bf16[1,64,128]{2,1,0:T(8,128)(2,1)S(1)}, u32[]{:S(2)}, u32[]{:S(2)}) collective-permute-start(bf16[1,64,128]{2,1,0:T(8,128)(2,1)S(1)} %get-tuple-element.89), channel_id=1, source_target_pairs={{0,1},{1,2},{2,3},{3,4},{4,5},{5,6},{6,7},{7,8},{8,9},{9,10},{10,1... | collective-permute-start | bytes 49160 | tf_op jit(solution)/shard_map/ppermute | solution.py:15
  15.3 0.9 copy-start.6
  16.4 10.0 %copy-start.5 = (s32[3]{0:T(128)S(1)}, s32[3]{0:T(128)}, u32[]{:S(2)}) copy-start(s32[3]{0:T(128)} %param.17) | copy-start | bytes 40
  16.5 16.4 %copy-start.3 = (bf16[32,128]{1,0:T(8,128)(2,1)S(1)}, bf16[32,128]{1,0:T(8,128)(2,1)}, u32[]{:S(2)}) copy-start(bf16[32,128]{1,0:T(8,128)(2,1)} %param.11) | copy-start | bytes 24580
  16.8 16.5 %copy-start.1 = (bf16[3,3,128,128]{3,2,1,0:T(8,128)(2,1)S(1)}, bf16[3,3,128,128]{3,2,1,0:T(8,128)(2,1)}, u32[]{:S(2)}) copy-start(bf16[3,3,128,128]{3,2,1,0:T(8,128)(2,1)} %param.14) | copy-start | bytes 884740
  18.5 14.6 %all-to-all-start = ((bf16[2,64,128]{2,0,1:T(2,128)(2,1)}), bf16[2,64,128]{2,0,1:T(2,128)(2,1)S(1)}, u32[]{:S(2)}, u32[]{:S(2)}) async-start(bf16[2,64,128]{2,0,1:T(2,128)(2,1)} %copy.1152), calls=%async_computation | async-start | bytes 65536 | tf_op jit(solution)/shard_map/all_to_all | solution.py:196
  33.8 1.1 copy-start.4
  47.6 12.6 %all-to-all-start.1 = ((bf16[16,2,4,128]{3,2,1,0:T(4,128)(2,1)}), bf16[16,2,4,128]{3,2,1,0:T(4,128)(2,1)S(1)}, u32[]{:S(2)}, u32[]{:S(2)}) async-start(bf16[16,2,4,128]{3,2,1,0:T(4,128)(2,1)} %constant_dynamic-update-slice_fusion), calls=%async_computation.1 | async-start | bytes 65536 | tf_op jit(solution)/shard_map/all_to_all | solution.py:202
  53.6 108.1 %all-reduce.15.cloned.1.call-start = ((), (), s32[]{:S(2)}) async-start(), calls=%async_computation.2 | async-start | bytes 2359296 | tf_op jit(solution)/shard_map/psum | solution.py:221
  61.5 6.8 %collective-permute-start.3 = (bf16[1,64,128]{2,1,0:T(8,128)(2,1)S(1)}, bf16[1,64,128]{2,1,0:T(8,128)(2,1)S(1)}, u32[]{:S(2)}, u32[]{:S(2)}) collective-permute-start(bf16[1,64,128]{2,1,0:T(8,128)(2,1)S(1)} %get-tuple-element.62), channel_id=1, source_target_pairs={{1,0},{2,1},{3,2},{4,3},{5,4},{6,5},{7,6},{8,7},{9,8},{10,9},{11,1... | collective-permute-start | bytes 49160 | tf_op jit(solution)/shard_map/ppermute | solution.py:16
  62.8 5.5 %collective-permute-start.2 = (bf16[1,64,128]{2,1,0:T(8,128)(2,1)S(1)}, bf16[1,64,128]{2,1,0:T(8,128)(2,1)S(1)}, u32[]{:S(2)}, u32[]{:S(2)}) collective-permute-start(bf16[1,64,128]{2,1,0:T(8,128)(2,1)S(1)} %get-tuple-element.61), channel_id=1, source_target_pairs={{0,1},{1,2},{2,3},{3,4},{4,5},{5,6},{6,7},{7,8},{8,9},{9,10},{10,1... | collective-permute-start | bytes 49160 | tf_op jit(solution)/shard_map/ppermute | solution.py:15
  161.7 2.0 %copy-start.2 = (f32[3,3,128,128]{3,2,1,0:T(8,128)S(1)}, f32[3,3,128,128]{3,2,1,0:T(8,128)}, u32[]{:S(2)}) copy-start(f32[3,3,128,128]{3,2,1,0:T(8,128)} %get-tuple-element.117) | copy-start | bytes 1769476
Sparse Core Ops, SparseCore 0:
  68.4 93.2 all-reduce.14
